TPU v7x, 32 devices: a whole 2x2x4 slice. The times are simulated.
32 devices in a mesh: stretch: 2 (over core), seq: 16 (over z, y, x).
Axes of the slice: x: 2, y: 2, z: 4, core: 2. Of those that a mesh axis runs over, the one named last changes fastest.
Arguments:
- queries: bfloat16 [4096, 1024], P(('stretch', 'seq')), may hold values from -16 to 16
- keys: bfloat16 [4096, 1024], P(('stretch', 'seq')), may hold values from -16 to 16
- values: bfloat16 [4096, 1024], P(('stretch', 'seq')), may hold values from -6 to 6
- tokens: bfloat16 [4096, 1536], P(('stretch', 'seq')), may hold values from -6 to 6
- out_weight: bfloat16 [1024, 1536], replicated, may hold values from -0.1875 to 0.1875
- gate_table: float32 [4, 1536], replicated, may hold values from 0.5 to 2
- timesteps: int32 [32], P(('stretch', 'seq')), may hold values from 0 to 3
Outputs:
- mixed: bfloat16 [4096, 1536], P(('stretch', 'seq'))
All inputs are finite; a program needn't handle non-finite values.
Results may differ from a plain program's by a relative error of at most 0.0051.
Values may be sent and summed in bfloat16 or wider, within the bound.
A program may use at most 128 MiB of HBM per device.

v0:
```python
import math

import jax
import jax.numpy as jnp
from jax import lax
from jax.sharding import PartitionSpec as P

HD = 128
HEADS = 8
SPAN = 3


def shifted(value, axis, steps):
    count = lax.axis_size(axis)
    initial, last = (max(0, -steps), min(count, count - steps))
    return lax.ppermute(value, axis, [(source, source + steps) for source in range(initial, last)])


def query_slots(block, quarters):
    count = block.shape[0]
    shaped = block.reshape(quarters, count // quarters, HEADS, HD)
    return shaped.transpose(2, 0, 1, 3).reshape(HEADS * quarters, 1, count // quarters, HD)


def cache_slots(stack, quarters):
    depth = stack.shape[0]
    count = stack.shape[1]
    shaped = stack.reshape(depth, count, HEADS, HD).transpose(2, 0, 1, 3)
    return jnp.repeat(shaped, quarters, axis=0)


def earlier_stretches(own_keys, own_values, prior):
    key_list = [own_keys]
    value_list = [own_values]
    for dist in range(1, prior + 1):
        moved = shifted((own_keys, own_values), "stretch", dist)
        key_list.append(moved[0])
        value_list.append(moved[1])
    return (key_list, value_list)


def on_device(queries, keys, values, tokens, out_weight, gate_table, timesteps):
    count = queries.shape[0]
    groups = lax.axis_size("seq")
    quarters = groups // HEADS
    rows_each = count // quarters
    stretch_id = lax.axis_index("stretch")
    prior = min(SPAN, lax.axis_size("stretch")) - 1
    q_slots = query_slots(queries, quarters)
    q_recv, k_recv, v_recv = (
        lax.all_to_all(q_slots, "seq", split_axis=0, concat_axis=2, tiled=True),
        lax.all_to_all(
            cache_slots(keys[None], quarters), "seq", split_axis=0, concat_axis=2, tiled=True
        ),
        lax.all_to_all(
            cache_slots(values[None], quarters), "seq", split_axis=0, concat_axis=2, tiled=True
        ),
    )
    key_list, value_list = earlier_stretches(k_recv.reshape(-1, HD), v_recv.reshape(-1, HD), prior)
    key_all = jnp.concatenate(key_list, axis=0)
    value_all = jnp.concatenate(value_list, axis=0)
    query_rows = q_recv.reshape(-1, HD)
    stretch_tok = groups * count
    slot_of = lax.iota(jnp.int32, key_all.shape[0]) // stretch_tok
    visible = slot_of <= stretch_id
    scale = 1.0 / math.sqrt(HD)
    total_rows = query_rows.shape[0]
    block = math.gcd(total_rows, 512)

    def attend(query_block):
        scores = (
            jnp.einsum("qd,kd->qk", query_block, key_all, preferred_element_type=jnp.float32)
            * scale
        )
        scores = jnp.where(visible[None, :], scores, -1e30)
        top = jnp.max(scores, axis=1, keepdims=True)
        expo = jnp.exp(scores - top)
        total = jnp.sum(expo, axis=1, keepdims=True)
        result = jnp.dot(expo.astype(jnp.bfloat16), value_all, preferred_element_type=jnp.float32)
        return (result / total).astype(jnp.bfloat16)

    attended = lax.map(attend, query_rows.reshape(total_rows // block, block, HD))
    attended = attended.reshape(groups, rows_each, HD)
    returned = lax.all_to_all(attended, "seq", split_axis=0, concat_axis=0, tiled=True)
    merged = (
        returned.reshape(HEADS, quarters, rows_each, HD)
        .transpose(1, 2, 0, 3)
        .reshape(count, HEADS * HD)
    )
    proj = jnp.dot(merged, out_weight, preferred_element_type=jnp.float32)
    mean_sq = jnp.mean(proj * proj, axis=1, keepdims=True)
    normed = proj * lax.rsqrt(mean_sq + 1e-06)
    own_step = timesteps[0]
    selector = lax.iota(jnp.int32, gate_table.shape[0]) == own_step
    gate = jnp.sum(jnp.where(selector[:, None], gate_table, 0.0), axis=0)
    return (tokens.astype(jnp.float32) + gate[None, :] * normed).astype(jnp.bfloat16)


def solution(mesh):
    in_specs = (
        P(("stretch", "seq"), None),
        P(("stretch", "seq"), None),
        P(("stretch", "seq"), None),
        P(("stretch", "seq"), None),
        P(),
        P(),
        P(("stretch", "seq")),
    )
    out_specs = P(("stretch", "seq"), None)
    return jax.shard_map(
        on_device, mesh=mesh, in_specs=in_specs, out_specs=out_specs, check_vma=False
    )
```

profile of v0, /device:TPU:0, one launch (start us, length us, event | category | flops | bytes accessed | tf_op | source)
XLA Modules:
  0.0 91.0 jit_solution(1615708255950900716)
XLA Ops:
  0.0 1.1 %copy.24 = bf16[16,8,8,128]{3,2,1,0:T(8,128)(2,1)S(1)} copy(bf16[16,8,8,128]{3,1,2,0:T(8,128)(2,1)} %bitcast.71) | data formatting | bytes 524288
  1.2 0.9 broadcast_in_dim.52
  2.1 8.4 %all-to-all-start.2 = ((bf16[16,1,128,128]{3,2,1,0:T(8,128)(2,1)}), bf16[16,1,128,128]{3,2,1,0:T(8,128)(2,1)}, u32[]{:S(2)}, u32[]{:S(2)}) async-start(bf16[16,1,128,128]{3,2,1,0:T(8,128)(2,1)} %bitcast.63), calls=%async_computation.2 | async-start | bytes 1048576 | tf_op jit(solution)/shard_map/all_to_all | solution.py:55
  10.5 1.0 %copy.23 = bf16[16,8,8,128]{3,2,1,0:T(8,128)(2,1)S(1)} copy(bf16[16,8,8,128]{3,1,2,0:T(8,128)(2,1)} %bitcast.72) | data formatting | bytes 524288
  11.6 14.1 %all-to-all-done.2 = bf16[16,1,128,128]{3,2,1,0:T(8,128)(2,1)} async-done(((bf16[16,1,128,128]{3,2,1,0:T(8,128)(2,1)}), bf16[16,1,128,128]{3,2,1,0:T(8,128)(2,1)}, u32[]{:S(2)}, u32[]{:S(2)}) %all-to-all-start.2) | async-done | bytes 524320 | tf_op jit(solution)/shard_map/all_to_all | solution.py:55
  25.7 0.9 broadcast_in_dim.50
  26.6 4.2 %all-to-all-start.1 = ((bf16[16,1,128,128]{3,2,1,0:T(8,128)(2,1)}), bf16[16,1,128,128]{3,2,1,0:T(8,128)(2,1)}, u32[]{:S(2)}, u32[]{:S(2)}) async-start(bf16[16,1,128,128]{3,2,1,0:T(8,128)(2,1)} %bitcast.64), calls=%async_computation.1 | async-start | bytes 1048576 | tf_op jit(solution)/shard_map/all_to_all | solution.py:52
  30.8 2.1 %collective-permute-start.1 = (bf16[2048,128]{1,0:T(8,128)(2,1)}, bf16[2048,128]{1,0:T(8,128)(2,1)}, u32[]{:S(2)}, u32[]{:S(2)}) collective-permute-start(bf16[2048,128]{1,0:T(8,128)(2,1)} %bitcast.11), channel_id=1, source_target_pairs={{0,16},{1,17},{2,18},{3,19},{4,20},{5,21},{6,22},{7,23},{8,24},{9,... | collective-permute-start | bytes 1572872 | tf_op jit(solution)/shard_map/ppermute | solution.py:16
  32.9 12.2 %all-to-all-done.1 = bf16[16,1,128,128]{3,2,1,0:T(8,128)(2,1)} async-done(((bf16[16,1,128,128]{3,2,1,0:T(8,128)(2,1)}), bf16[16,1,128,128]{3,2,1,0:T(8,128)(2,1)}, u32[]{:S(2)}, u32[]{:S(2)}) %all-to-all-start.1) | async-done | bytes 524320 | tf_op jit(solution)/shard_map/all_to_all | solution.py:52
  45.1 2.1 %collective-permute-start = (bf16[2048,128]{1,0:T(8,128)(2,1)}, bf16[2048,128]{1,0:T(8,128)(2,1)}, u32[]{:S(2)}, u32[]{:S(2)}) collective-permute-start(bf16[2048,128]{1,0:T(8,128)(2,1)} %bitcast.7), channel_id=1, source_target_pairs={{0,16},{1,17},{2,18},{3,19},{4,20},{5,21},{6,22},{7,23},{8,24},{9,... | collective-permute-start | bytes 1572872 | tf_op jit(solution)/shard_map/ppermute | solution.py:16
  47.2 1.0 %copy.22 = bf16[16,8,8,128]{3,2,1,0:T(8,128)(2,1)S(1)} copy(bf16[16,8,8,128]{3,1,2,0:T(8,128)(2,1)} %bitcast.73) | data formatting | bytes 524288
  48.2 0.8 copy.18
  48.9 3.8 %all-to-all-start = ((bf16[16,1,64,128]{3,2,1,0:T(8,128)(2,1)}), bf16[16,1,64,128]{3,2,1,0:T(8,128)(2,1)S(1)}, u32[]{:S(2)}, u32[]{:S(2)}) async-start(bf16[16,1,64,128]{3,2,1,0:T(8,128)(2,1)} %bitcast.66), calls=%async_computation | async-start | bytes 524288 | tf_op jit(solution)/shard_map/all_to_all | solution.py:51
  52.8 0.0 collective-permute-done.1
  52.8 2.2 %pad_maximum_fusion.1 = bf16[4096,128]{1,0:T(8,128)(2,1)} fusion(bf16[2048,128]{1,0:T(8,128)(2,1)} %collective-permute-done.1, bf16[2048,128]{1,0:T(8,128)(2,1)} %bitcast.11), kind=kLoop, calls=%fused_computation.27 | loop fusion | flops 2097152 | bytes 2097152 | tf_op jit(solution)/shard_map/concatenate | solution.py:61
  55.0 0.0 collective-permute-done
  55.0 2.3 %pad_maximum_fusion = bf16[4096,128]{1,0:T(8,128)(2,1)} fusion(bf16[2048,128]{1,0:T(8,128)(2,1)} %collective-permute-done, bf16[2048,128]{1,0:T(8,128)(2,1)} %bitcast.7), kind=kLoop, calls=%fused_computation.26 | loop fusion | flops 2097152 | bytes 2097152 | tf_op jit(solution)/shard_map/concatenate | solution.py:60
  57.3 4.0 %all-to-all-done = bf16[16,1,64,128]{3,2,1,0:T(8,128)(2,1)S(1)} async-done(((bf16[16,1,64,128]{3,2,1,0:T(8,128)(2,1)}), bf16[16,1,64,128]{3,2,1,0:T(8,128)(2,1)S(1)}, u32[]{:S(2)}, u32[]{:S(2)}) %all-to-all-start) | async-done | bytes 262176 | tf_op jit(solution)/shard_map/all_to_all | solution.py:51
  61.3 14.8 %while.11 = (s32[]{:T(128)}, bf16[2,512,128]{2,1,0:T(8,128)(2,1)}, bf16[2,512,128]{2,1,0:T(8,128)(2,1)S(1)}, bf16[4096,128]{1,0:T(8,128)(2,1)}, bf16[4096,128]{1,0:T(8,128)(2,1)}, /*index=5*/s32[]{:T(128)}, s32[]{:T(128)}) while((s32[]{:T(128)}, bf16[2,512,128]{2,1,0:T(8,128)(2,1)}, bf16[2,512,128]{2,1,0:T(8,128)(2,1)S(1)}, ...), condition=%wide.region_4.5_spmd.clone, body=%wide.region_1.4_spmd.clone.sunk | while | flops 1096977408 | bytes 31746672 | solution.py:82
  61.3 2.8 %fusion.47 = (f32[512]{0:T(512)S(1)}, f32[512,4096]{1,0:T(8,128)S(1)}) fusion(pred[4096]{0:T(1024)(128)(4,1)S(1)} %fusion.46, bf16[4096,128]{1,0:T(8,128)(2,1)} %get-tuple-element.127, bf16[2,512,128]{2,1,0:T(8,128)(2,1)S(1)} %get-tuple-element.126, s32[]{:T(128)} %get-tuple-element.117), kind=kOutput, calls=%fused_computation.3.clone.1 | convolution fusion | flops 543161856 | bytes 9574404 | tf_op jit(solution)/shard_map/while/body/eval_jaxpr/qd,kd->qk/dot_general | solution.py:72
  64.1 2.2 %fusion.48 = f32[512]{0:T(512)S(1)} fusion(f32[512,4096]{1,0:T(8,128)S(1)} %get-tuple-element.108, f32[512]{0:T(512)S(1)} %get-tuple-element.109, pred[4096]{0:T(1024)(128)(4,1)S(1)} %fusion.46), kind=kLoop, calls=%fused_computation.4.clone.1 | loop fusion | flops 8388096 | bytes 8396800 | tf_op jit(solution)/shard_map/while/body/eval_jaxpr/reduce_sum | solution.py:78
  66.3 2.4 %fusion.49 = bf16[2,512,128]{2,1,0:T(8,128)(2,1)} fusion(bf16[2,512,128]{2,1,0:T(8,128)(2,1)} %get-tuple-element.118, s32[]{:T(128)} %get-tuple-element.117, bf16[4096,128]{1,0:T(8,128)(2,1)S(1)} %copy-done.1, f32[512,4096]{1,0:T(8,128)S(1)} %get-tuple-element.108, f32[512]{0:T(512)S(1)} %get-tuple-element.109, pred[4096]{0:T(1024)(128)(4,1)S(1)} %fusion.46, ...), kind=kOutput, calls=%fused_computation.11.clone.1 | convolution fusion | flops 545390592 | bytes 9576960 | tf_op jit(solution)/shard_map/while/body/eval_jaxpr/dot_general | solution.py:79
  68.7 2.8 %fusion.47 = (f32[512]{0:T(512)S(1)}, f32[512,4096]{1,0:T(8,128)S(1)}) fusion(pred[4096]{0:T(1024)(128)(4,1)S(1)} %fusion.46, bf16[4096,128]{1,0:T(8,128)(2,1)} %get-tuple-element.127, bf16[2,512,128]{2,1,0:T(8,128)(2,1)S(1)} %get-tuple-element.126, s32[]{:T(128)} %get-tuple-element.117), kind=kOutput, calls=%fused_computation.3.clone.1 | convolution fusion | flops 543161856 | bytes 9574404 | tf_op jit(solution)/shard_map/while/body/eval_jaxpr/qd,kd->qk/dot_general | solution.py:72
  71.5 2.2 %fusion.48 = f32[512]{0:T(512)S(1)} fusion(f32[512,4096]{1,0:T(8,128)S(1)} %get-tuple-element.108, f32[512]{0:T(512)S(1)} %get-tuple-element.109, pred[4096]{0:T(1024)(128)(4,1)S(1)} %fusion.46), kind=kLoop, calls=%fused_computation.4.clone.1 | loop fusion | flops 8388096 | bytes 8396800 | tf_op jit(solution)/shard_map/while/body/eval_jaxpr/reduce_sum | solution.py:78
  73.7 2.4 %fusion.49 = bf16[2,512,128]{2,1,0:T(8,128)(2,1)} fusion(bf16[2,512,128]{2,1,0:T(8,128)(2,1)} %get-tuple-element.118, s32[]{:T(128)} %get-tuple-element.117, bf16[4096,128]{1,0:T(8,128)(2,1)S(1)} %copy-done.1, f32[512,4096]{1,0:T(8,128)S(1)} %get-tuple-element.108, f32[512]{0:T(512)S(1)} %get-tuple-element.109, pred[4096]{0:T(1024)(128)(4,1)S(1)} %fusion.46, ...), kind=kOutput, calls=%fused_computation.11.clone.1 | convolution fusion | flops 545390592 | bytes 9576960 | tf_op jit(solution)/shard_map/while/body/eval_jaxpr/dot_general | solution.py:79
  76.1 3.5 %all-to-all-start.3 = ((bf16[16,64,128]{2,1,0:T(8,128)(2,1)}), bf16[16,64,128]{2,1,0:T(8,128)(2,1)S(1)}, u32[]{:S(2)}, u32[]{:S(2)}) async-start(bf16[16,64,128]{2,1,0:T(8,128)(2,1)} %bitcast.12), calls=%async_computation.3 | async-start | bytes 524288 | tf_op jit(solution)/shard_map/all_to_all | solution.py:84
  80.3 0.1 select_reduce_fusion
  80.4 7.7 %all-to-all-done.3 = bf16[16,64,128]{2,1,0:T(8,128)(2,1)S(1)} async-done(((bf16[16,64,128]{2,1,0:T(8,128)(2,1)}), bf16[16,64,128]{2,1,0:T(8,128)(2,1)S(1)}, u32[]{:S(2)}, u32[]{:S(2)}) %all-to-all-start.3) | async-done | bytes 262176 | tf_op jit(solution)/shard_map/all_to_all | solution.py:84
  88.2 0.2 copy.21
  88.3 0.0 copy-done
  88.3 0.7 multiply_reduce_fusion
  89.0 1.9 %add_convert_fusion = bf16[128,1536]{1,0:T(8,128)(2,1)} fusion(f32[128,1536]{1,0:T(8,128)S(1)} %get-tuple-element.68, bf16[128,1536]{1,0:T(8,128)(2,1)} %param.12, f32[128]{0:T(128)S(1)} %add_rsqrt_fusion, f32[1536]{0:T(1024)S(1)} %select_reduce_fusion), kind=kLoop, calls=%fused_computation.28 | loop fusion | flops 983040 | bytes 1579520 | tf_op jit(solution)/shard_map/convert_element_type | solution.py:96
  (16 shorter events, 0.2 us)
Async XLA Ops:
  0.0 88.3 %copy-start = (bf16[1024,1536]{1,0:T(8,128)(2,1)S(1)}, bf16[1024,1536]{1,0:T(8,128)(2,1)}, u32[]{:S(2)}) copy-start(bf16[1024,1536]{1,0:T(8,128)(2,1)} %param.13) | copy-start | bytes 9437188
  2.1 23.5 %all-to-all-start.2 = ((bf16[16,1,128,128]{3,2,1,0:T(8,128)(2,1)}), bf16[16,1,128,128]{3,2,1,0:T(8,128)(2,1)}, u32[]{:S(2)}, u32[]{:S(2)}) async-start(bf16[16,1,128,128]{3,2,1,0:T(8,128)(2,1)} %bitcast.63), calls=%async_computation.2 | async-start | bytes 1048576 | tf_op jit(solution)/shard_map/all_to_all | solution.py:55
  26.6 18.5 %all-to-all-start.1 = ((bf16[16,1,128,128]{3,2,1,0:T(8,128)(2,1)}), bf16[16,1,128,128]{3,2,1,0:T(8,128)(2,1)}, u32[]{:S(2)}, u32[]{:S(2)}) async-start(bf16[16,1,128,128]{3,2,1,0:T(8,128)(2,1)} %bitcast.64), calls=%async_computation.1 | async-start | bytes 1048576 | tf_op jit(solution)/shard_map/all_to_all | solution.py:52
  30.8 22.0 %collective-permute-start.1 = (bf16[2048,128]{1,0:T(8,128)(2,1)}, bf16[2048,128]{1,0:T(8,128)(2,1)}, u32[]{:S(2)}, u32[]{:S(2)}) collective-permute-start(bf16[2048,128]{1,0:T(8,128)(2,1)} %bitcast.11), channel_id=1, source_target_pairs={{0,16},{1,17},{2,18},{3,19},{4,20},{5,21},{6,22},{7,23},{8,24},{9,... | collective-permute-start | bytes 1572872 | tf_op jit(solution)/shard_map/ppermute | solution.py:16
  45.1 10.0 %collective-permute-start = (bf16[2048,128]{1,0:T(8,128)(2,1)}, bf16[2048,128]{1,0:T(8,128)(2,1)}, u32[]{:S(2)}, u32[]{:S(2)}) collective-permute-start(bf16[2048,128]{1,0:T(8,128)(2,1)} %bitcast.7), channel_id=1, source_target_pairs={{0,16},{1,17},{2,18},{3,19},{4,20},{5,21},{6,22},{7,23},{8,24},{9,... | collective-permute-start | bytes 1572872 | tf_op jit(solution)/shard_map/ppermute | solution.py:16
  48.9 12.4 %all-to-all-start = ((bf16[16,1,64,128]{3,2,1,0:T(8,128)(2,1)}), bf16[16,1,64,128]{3,2,1,0:T(8,128)(2,1)S(1)}, u32[]{:S(2)}, u32[]{:S(2)}) async-start(bf16[16,1,64,128]{3,2,1,0:T(8,128)(2,1)} %bitcast.66), calls=%async_computation | async-start | bytes 524288 | tf_op jit(solution)/shard_map/all_to_all | solution.py:51
  61.3 19.0 %copy-start.2 = (f32[4,1536]{1,0:T(4,128)S(1)}, f32[4,1536]{1,0:T(4,128)}, u32[]{:S(2)}) copy-start(f32[4,1536]{1,0:T(4,128)} %param.14) | copy-start | bytes 73732
  61.3 5.0 %copy-start.1 = (bf16[4096,128]{1,0:T(8,128)(2,1)S(1)}, bf16[4096,128]{1,0:T(8,128)(2,1)}, u32[]{:S(2)}) copy-start(bf16[4096,128]{1,0:T(8,128)(2,1)} %get-tuple-element.128) | copy-start | bytes 3145732 | tf_op jit(solution)/shard_map/while
  68.7 5.0 %copy-start.1 = (bf16[4096,128]{1,0:T(8,128)(2,1)S(1)}, bf16[4096,128]{1,0:T(8,128)(2,1)}, u32[]{:S(2)}) copy-start(bf16[4096,128]{1,0:T(8,128)(2,1)} %get-tuple-element.128) | copy-start | bytes 3145732 | tf_op jit(solution)/shard_map/while
  76.1 12.0 %all-to-all-start.3 = ((bf16[16,64,128]{2,1,0:T(8,128)(2,1)}), bf16[16,64,128]{2,1,0:T(8,128)(2,1)S(1)}, u32[]{:S(2)}, u32[]{:S(2)}) async-start(bf16[16,64,128]{2,1,0:T(8,128)(2,1)} %bitcast.12), calls=%async_computation.3 | async-start | bytes 524288 | tf_op jit(solution)/shard_map/all_to_all | solution.py:84
where the time goes:
time: 91.7 us; the launch traced here: 91 us
  waiting for transfers between devices  37.9 us (41%)
  starting transfers between devices  24.2 us (26%)
  matrix products  11.1 us (12%)
  other arithmetic  10.9 us (12%)
  local copies, waits for them, and re-layouts  5.99 us (7%)
    all_to_all x1, waiting for transfers between devices, on_device(): lax.all_to_all(cache_slots(values[None], quarters), 'seq', split_axis=0,...  14.1 us
    all_to_all x1, waiting for transfers between devices, on_device(): lax.all_to_all(cache_slots(keys[None], quarters), 'seq', split_axis=0, co...  12.2 us
    all_to_all x1, starting transfers between devices, on_device(): lax.all_to_all(cache_slots(values[None], quarters), 'seq', split_axis=0,...  8.39 us
    all_to_all x1, waiting for transfers between devices, on_device(): lax.all_to_all(attended, 'seq', split_axis=0, concat_axis=0, tiled=True)  7.72 us
    dot_general x2, matrix products, attend(): jnp.einsum('qd,kd->qk', query_block, key_all, preferred_element_type=jnp....  5.56 us
    dot_general x2, matrix products, attend(): jnp.dot(expo.astype(jnp.bfloat16), value_all, preferred_element_type=jnp....  4.9 us
    reduce_sum x2, other arithmetic, attend(): total = jnp.sum(expo, axis=1, keepdims=True)  4.33 us
    all_to_all x1, starting transfers between devices, on_device(): lax.all_to_all(cache_slots(keys[None], quarters), 'seq', split_axis=0, co...  4.25 us
  transfers between devices with their start and end apart: 6, of which 4 were waited for; matrix products, arithmetic and copies ran while one was open for 8% of the time, Pallas kernels for 0%

commit v1 on v0

v1 whole, which is shorter than its diff:
```python
import functools
import math

import jax
import jax.numpy as jnp
from jax import lax
from jax.experimental import pallas as pl
from jax.experimental.pallas import tpu as pltpu
from jax.sharding import PartitionSpec as P

HD = 128
HEADS = 8
SPAN = 3
MESH = pl.DeviceIdType.MESH


def kernel(groups, stretches, chunk, q_ref, k_ref, v_ref, tok_ref, w_ref, gate_ref, step_ref, out_ref,
           qbuf, kbuf, vbuf, kprior, vprior, top_s, sum_s, acc_s, obuf, att, w_s, tok_s,
           load_sem, local_sem, q_send, q_recv, kv_send, k_recv, v_recv,
           fwd_send, kp_recv, vp_recv, o_send, o_recv):
    count = q_ref.shape[0]
    prior = min(SPAN, stretches) - 1
    chunks = groups // chunk
    stretch = lax.axis_index("stretch")
    me = lax.axis_index("seq")
    head = lax.rem(me, HEADS)
    share = me // HEADS

    def cols(index):
        return pl.ds(pl.multiple_of(index * HD, HD), HD)

    w_copy = pltpu.make_async_copy(w_ref, w_s, load_sem.at[0])
    tok_copy = pltpu.make_async_copy(tok_ref, tok_s, load_sem.at[1])
    own = [
        pltpu.make_async_copy(q_ref.at[:, cols(head)], qbuf.at[head], local_sem.at[0]),
        pltpu.make_async_copy(k_ref.at[:, cols(head)], kbuf.at[me], local_sem.at[1]),
        pltpu.make_async_copy(v_ref.at[:, cols(head)], vbuf.at[me], local_sem.at[2]),
    ]

    barrier = pltpu.get_barrier_semaphore()

    @pl.loop(1, groups)
    def _(off):
        peer = lax.rem(me + off, groups)
        pl.semaphore_signal(barrier, inc=1, device_id=(stretch, peer), device_id_type=MESH)

    for dist in range(1, prior + 1):
        @pl.when(stretch + dist < stretches)
        def _():
            pl.semaphore_signal(barrier, inc=1, device_id=(stretch + dist, me), device_id_type=MESH)

        @pl.when(stretch >= dist)
        def _():
            pl.semaphore_signal(barrier, inc=1, device_id=(stretch - dist, me), device_id_type=MESH)

    for copy in own:
        copy.start()
    w_copy.start()
    tok_copy.start()
    partners = jnp.minimum(stretch, prior) + jnp.minimum(stretches - 1 - stretch, prior)
    pl.semaphore_wait(barrier, groups - 1 + partners)

    def q_copy(off):
        other = lax.rem(head + off, HEADS)
        return pltpu.make_async_remote_copy(
            src_ref=q_ref.at[:, cols(other)], dst_ref=qbuf.at[head],
            send_sem=q_send.at[other], recv_sem=q_recv.at[head],
            device_id=(stretch, share * HEADS + other), device_id_type=MESH)

    def kv_copy(index, which):
        off = 1 + lax.rem(groups // 2 - 1 + index, groups - 1)
        peer = lax.rem(me + off, groups)
        src, dst, recv = ((k_ref, kbuf, k_recv), (v_ref, vbuf, v_recv))[which]
        return pltpu.make_async_remote_copy(
            src_ref=src.at[:, cols(lax.rem(peer, HEADS))], dst_ref=dst.at[me],
            send_sem=kv_send.at[which, peer], recv_sem=recv.at[me],
            device_id=(stretch, peer), device_id_type=MESH)

    @pl.loop(1, HEADS)
    def _(off):
        q_copy(off).start()

    @pl.loop(0, groups - 1)
    def _(index):
        kv_copy(index, 0).start()
        kv_copy(index, 1).start()

    top_s[...] = jnp.full_like(top_s, -1e30)
    sum_s[...] = jnp.zeros_like(sum_s)
    acc_s[...] = jnp.zeros_like(acc_s)

    for copy in own:
        copy.wait()

    def arrived(buf, sems, slot, sends):
        return pltpu.make_async_remote_copy(
            src_ref=buf.at[slot], dst_ref=buf.at[slot], send_sem=sends, recv_sem=sems.at[slot],
            device_id=(stretch, lax.rem(me + 1, groups)), device_id_type=MESH)

    @pl.loop(1, HEADS)
    def _(off):
        arrived(qbuf, q_recv, lax.rem(head + off, HEADS), q_send.at[0]).wait_recv()

    factor = math.log2(math.e) / math.sqrt(HD)
    keys_each = chunk * count
    per = 2 if HEADS % 2 == 0 else 1
    rows = per * count

    def absorb(key_ref, value_ref):
        key_block = key_ref[...].reshape(keys_each, HD)
        value_block = value_ref[...].reshape(keys_each, HD)
        for block in range(HEADS // per):
            span = pl.ds(block * rows, rows)
            query = qbuf[pl.ds(block * per, per)].reshape(rows, HD)
            scores = lax.dot_general(query, key_block, (((1,), (1,)), ((), ())),
                                     preferred_element_type=jnp.float32)
            old = top_s[span, :]
            new = jnp.maximum(old, jnp.max(scores, axis=1, keepdims=True))
            top_s[span, :] = new
            fade = jnp.exp2((old - new) * factor)
            weights = [
                jnp.exp2((scores[:, part * HD:(part + 1) * HD] - new) * factor)
                for part in range(keys_each // HD)
            ]
            sum_s[span, :] = sum_s[span, :] * fade + functools.reduce(jnp.add, weights)
            expo = jnp.concatenate([part.astype(jnp.bfloat16) for part in weights], axis=1)
            acc_s[span, :] = acc_s[span, :] * fade + jnp.dot(
                expo, value_block, preferred_element_type=jnp.float32)

    def forward(first, slot, dist, which):
        src, dst, recv = ((kbuf, kprior, kp_recv), (vbuf, vprior, vp_recv))[which]
        return pltpu.make_async_remote_copy(
            src_ref=src.at[pl.ds(first, chunk)], dst_ref=dst.at[dist - 1, pl.ds(first, chunk)],
            send_sem=fwd_send.at[which, dist - 1, slot], recv_sem=recv.at[dist - 1, slot],
            device_id=(stretch + dist, me), device_id_type=MESH)

    my_chunk = me // chunk
    low = my_chunk < chunks // 2

    def chunk_at(index):
        rising = lax.rem(my_chunk + index, chunks)
        falling = lax.rem(my_chunk + chunks - index, chunks)
        return jnp.where(low, rising, falling)

    @pl.loop(0, chunks)
    def _(index):
        slot = chunk_at(index)
        first = slot * chunk
        for step in range(chunk):
            source = first + step

            @pl.when(source != me)
            def _():
                arrived(kbuf, k_recv, source, kv_send.at[0, 0]).wait_recv()
                arrived(vbuf, v_recv, source, kv_send.at[0, 0]).wait_recv()

        for dist in range(1, prior + 1):
            @pl.when(stretch + dist < stretches)
            def _():
                forward(first, slot, dist, 0).start()
                forward(first, slot, dist, 1).start()

        absorb(kbuf.at[pl.ds(first, chunk)], vbuf.at[pl.ds(first, chunk)])
        for dist in range(1, prior + 1):
            @pl.when(stretch >= dist)
            def _():
                for which in range(2):
                    src, recv = ((kprior, kp_recv), (vprior, vp_recv))[which]
                    pltpu.make_async_remote_copy(
                        src_ref=src.at[dist - 1, pl.ds(first, chunk)],
                        dst_ref=src.at[dist - 1, pl.ds(first, chunk)],
                        send_sem=fwd_send.at[which, dist - 1, slot], recv_sem=recv.at[dist - 1, slot],
                        device_id=(stretch - dist, me), device_id_type=MESH).wait_recv()
                absorb(kprior.at[dist - 1, pl.ds(first, chunk)], vprior.at[dist - 1, pl.ds(first, chunk)])

    for source in range(HEADS):
        span = pl.ds(source * count, count)
        total = jnp.sum(sum_s[span, :], axis=1, keepdims=True)
        obuf[source] = (acc_s[span, :] / total).astype(jnp.bfloat16)

    def o_copy(off):
        other = lax.rem(head + off, HEADS)
        return pltpu.make_async_remote_copy(
            src_ref=obuf.at[other], dst_ref=att.at[:, cols(head)],
            send_sem=o_send.at[other], recv_sem=o_recv.at[head],
            device_id=(stretch, share * HEADS + other), device_id_type=MESH)

    @pl.loop(1, HEADS)
    def _(off):
        o_copy(off).start()

    own_out = pltpu.make_async_copy(obuf.at[head], att.at[:, cols(head)], local_sem.at[0])
    own_out.start()
    w_copy.wait()
    tok_copy.wait()

    table = gate_ref[...]
    picked = lax.broadcasted_iota(jnp.int32, table.shape, 0) == step_ref[0]
    gate = jnp.sum(jnp.where(picked, table, 0.0), axis=0, keepdims=True)

    own_out.wait()

    @pl.loop(1, HEADS)
    def _(off):
        other = lax.rem(head + off, HEADS)
        pltpu.make_async_remote_copy(
            src_ref=obuf.at[other], dst_ref=att.at[:, cols(other)],
            send_sem=o_send.at[other], recv_sem=o_recv.at[other],
            device_id=(stretch, share * HEADS + other), device_id_type=MESH).wait_recv()

    proj = jnp.dot(att[...], w_s[...], preferred_element_type=jnp.float32)
    mean_sq = jnp.mean(proj * proj, axis=1, keepdims=True)
    normed = proj * lax.rsqrt(mean_sq + 1e-06)
    out_ref[...] = (tok_s[...].astype(jnp.float32) + gate * normed).astype(jnp.bfloat16)

    @pl.loop(1, HEADS)
    def _(off):
        q_copy(off).wait_send()
        o_copy(off).wait_send()

    @pl.loop(0, groups - 1)
    def _(index):
        kv_copy(index, 0).wait_send()
        kv_copy(index, 1).wait_send()

    for dist in range(1, prior + 1):
        @pl.when(stretch + dist < stretches)
        def _():
            @pl.loop(0, chunks)
            def _(slot):
                forward(slot * chunk, slot, dist, 0).wait_send()
                forward(slot * chunk, slot, dist, 1).wait_send()


def solution(mesh):
    stretches, groups = mesh.shape["stretch"], mesh.shape["seq"]
    prior = max(1, min(SPAN, stretches) - 1)
    chunk = math.gcd(groups, 4)

    def on_device(queries, keys, values, tokens, out_weight, gate_table, timesteps):
        count = queries.shape[0]
        block = (count, HD)
        dma = pltpu.SemaphoreType.DMA
        anywhere = pl.BlockSpec(memory_space=pl.ANY)
        vmem = pl.BlockSpec(memory_space=pltpu.VMEM)
        rows = HEADS * count
        return pl.pallas_call(
            functools.partial(kernel, groups, stretches, chunk),
            out_shape=jax.ShapeDtypeStruct(tokens.shape, jnp.bfloat16),
            in_specs=[anywhere] * 5 + [vmem, pl.BlockSpec(memory_space=pltpu.SMEM)],
            out_specs=vmem,
            scratch_shapes=[
                pltpu.VMEM((HEADS, *block), jnp.bfloat16),
                pltpu.VMEM((groups, *block), jnp.bfloat16),
                pltpu.VMEM((groups, *block), jnp.bfloat16),
                pltpu.VMEM((prior, groups, *block), jnp.bfloat16),
                pltpu.VMEM((prior, groups, *block), jnp.bfloat16),
                pltpu.VMEM((rows, HD), jnp.float32),
                pltpu.VMEM((rows, HD), jnp.float32),
                pltpu.VMEM((rows, HD), jnp.float32),
                pltpu.VMEM((HEADS, *block), jnp.bfloat16),
                pltpu.VMEM((count, HEADS * HD), jnp.bfloat16),
                pltpu.VMEM(out_weight.shape, jnp.bfloat16),
                pltpu.VMEM(tokens.shape, jnp.bfloat16),
                dma((2,)),
                dma((3,)),
                dma((HEADS,)),
                dma((HEADS,)),
                dma((2, groups)),
                dma((groups,)),
                dma((groups,)),
                dma((2, prior, groups // chunk)),
                dma((prior, groups // chunk)),
                dma((prior, groups // chunk)),
                dma((HEADS,)),
                dma((HEADS,)),
            ],
            compiler_params=pltpu.CompilerParams(collective_id=0, has_side_effects=True),
        )(queries, keys, values, tokens, out_weight, gate_table, timesteps)

    row = P(("stretch", "seq"), None)
    return jax.shard_map(
        on_device, mesh=mesh,
        in_specs=(row, row, row, row, P(), P(), P(("stretch", "seq"))),
        out_specs=row, check_vma=False)
```

time: 91.7 us -> 49 us (0.53)
  the two profiles are of different devices: /device:TPU:0 before, /device:TPU:1 now
where the time goes in v1:
time: 49 us; the launch traced here: 48.7 us
  Pallas kernels  46.3 us (94%)
  local copies, waits for them, and re-layouts  1.77 us (4%)
  between operations  0.66 us (1%)
    pallas_call x1, Pallas kernels, on_device(): pl.pallas_call(functools.partial(kernel, groups, stretches, chunk), out_s...  46.3 us
    unnamed x1, local copies, waits for them, and re-layouts  1.77 us

profile of v1, /device:TPU:1, one launch (start us, length us, event | category | flops | bytes accessed | tf_op | source)
XLA Modules:
  0.0 48.7 jit_solution(10720901085545485709)
XLA Ops:
  0.7 46.3 %shard_map.73 = bf16[128,1536]{1,0:T(8,128)(2,1)} custom-call(bf16[128,1024]{1,0:T(8,128)(2,1)} %q_ref.1, bf16[128,1024]{1,0:T(8,128)(2,1)} %k_ref.1, bf16[128,1024]{1,0:T(8,128)(2,1)} %v_ref.1, bf16[128,1536]{1,0:T(8,128)(2,1)} %tok_ref.1, bf16[1024,1536]{1,0:T(8,128)(2,1)} %w_ref.1, f32[4,1536]{1,0:T(4,128)} %gate_ref.1, s32[1]{0:T(128)S(6)} %copy.9.step_ref), custom_call_target="tpu_custom_call" | custom-call | tf_op jit(solution)/shard_map/pallas_call | solution.py:247
  47.0 1.8 %copy.10 = bf16[128,1536]{1,0:T(8,128)(2,1)} copy(bf16[128,1536]{1,0:T(8,128)(2,1)} %shard_map.73) | data formatting | bytes 786432

commit v2 on v1

--- a/solution.py
+++ b/solution.py
@@ -14,13 +14,35 @@
 MESH = pl.DeviceIdType.MESH
 
 
+def flip(base, mask):
+    result = base
+    for bit in range(mask.bit_length()):
+        step = 1 << bit
+        if mask & step:
+            result = result + step * (1 - 2 * lax.rem(lax.div(base, step), 2))
+    return result
+
+
+def rounds_of(bits):
+    known = {0} | {1 << bit for bit in range(bits)}
+    rounds = [sorted(known - {0}, reverse=True)]
+    for bit in range(bits):
+        fresh = {mask ^ (1 << bit) for mask in known} - known
+        if not fresh:
+            break
+        rounds.append(sorted(fresh, reverse=True))
+        known |= fresh
+    return rounds
+
+
 def kernel(groups, stretches, chunk, q_ref, k_ref, v_ref, tok_ref, w_ref, gate_ref, step_ref, out_ref,
            qbuf, kbuf, vbuf, kprior, vprior, top_s, sum_s, acc_s, obuf, att, w_s, tok_s,
            load_sem, local_sem, q_send, q_recv, kv_send, k_recv, v_recv,
-           fwd_send, kp_recv, vp_recv, o_send, o_recv):
+           fwd_send, kp_recv, vp_recv, o_send, o_recv, ready):
     count = q_ref.shape[0]
     prior = min(SPAN, stretches) - 1
     chunks = groups // chunk
+    bits = groups.bit_length() - 1
     stretch = lax.axis_index("stretch")
     me = lax.axis_index("seq")
     head = lax.rem(me, HEADS)
@@ -39,11 +61,8 @@
 
     barrier = pltpu.get_barrier_semaphore()
 
-    @pl.loop(1, groups)
-    def _(off):
-        peer = lax.rem(me + off, groups)
-        pl.semaphore_signal(barrier, inc=1, device_id=(stretch, peer), device_id_type=MESH)
-
+    for bit in range(bits):
+        pl.semaphore_signal(barrier, inc=1, device_id=(stretch, flip(me, 1 << bit)), device_id_type=MESH)
     for dist in range(1, prior + 1):
         @pl.when(stretch + dist < stretches)
         def _():
@@ -58,32 +77,33 @@
     w_copy.start()
     tok_copy.start()
     partners = jnp.minimum(stretch, prior) + jnp.minimum(stretches - 1 - stretch, prior)
-    pl.semaphore_wait(barrier, groups - 1 + partners)
-
-    def q_copy(off):
-        other = lax.rem(head + off, HEADS)
-        return pltpu.make_async_remote_copy(
-            src_ref=q_ref.at[:, cols(other)], dst_ref=qbuf.at[head],
-            send_sem=q_send.at[other], recv_sem=q_recv.at[head],
-            device_id=(stretch, share * HEADS + other), device_id_type=MESH)
-
-    def kv_copy(index, which):
-        off = 1 + lax.rem(groups // 2 - 1 + index, groups - 1)
-        peer = lax.rem(me + off, groups)
+    pl.semaphore_wait(barrier, bits + partners)
+
+    def q_copy(mask):
+        peer = flip(me, mask)
+        return pltpu.make_async_remote_copy(
+            src_ref=q_ref.at[:, cols(lax.rem(peer, HEADS))], dst_ref=qbuf.at[head],
+            send_sem=q_send.at[mask], recv_sem=q_recv.at[head],
+            device_id=(stretch, peer), device_id_type=MESH)
+
+    def kv_copy(mask, which):
+        peer = flip(me, mask)
         src, dst, recv = ((k_ref, kbuf, k_recv), (v_ref, vbuf, v_recv))[which]
         return pltpu.make_async_remote_copy(
             src_ref=src.at[:, cols(lax.rem(peer, HEADS))], dst_ref=dst.at[me],
-            send_sem=kv_send.at[which, peer], recv_sem=recv.at[me],
+            send_sem=kv_send.at[which, mask], recv_sem=recv.at[me],
             device_id=(stretch, peer), device_id_type=MESH)
 
-    @pl.loop(1, HEADS)
-    def _(off):
-        q_copy(off).start()
-
-    @pl.loop(0, groups - 1)
-    def _(index):
-        kv_copy(index, 0).start()
-        kv_copy(index, 1).start()
+    for turn, masks in enumerate(rounds_of(bits)):
+        if turn:
+            near = flip(me, 1 << (turn - 1))
+            pl.semaphore_signal(ready.at[turn - 1], inc=1, device_id=(stretch, near), device_id_type=MESH)
+            pl.semaphore_wait(ready.at[turn - 1], 1)
+        for mask in masks:
+            if mask < HEADS:
+                q_copy(mask).start()
+            kv_copy(mask, 0).start()
+            kv_copy(mask, 1).start()
 
     top_s[...] = jnp.full_like(top_s, -1e30)
     sum_s[...] = jnp.zeros_like(sum_s)
@@ -103,29 +123,32 @@
 
     factor = math.log2(math.e) / math.sqrt(HD)
     keys_each = chunk * count
-    per = 2 if HEADS % 2 == 0 else 1
+    per = math.gcd(HEADS, 4)
     rows = per * count
 
-    def absorb(key_ref, value_ref):
+    def absorb_block(block, key_ref, value_ref):
         key_block = key_ref[...].reshape(keys_each, HD)
         value_block = value_ref[...].reshape(keys_each, HD)
+        span = pl.ds(pl.multiple_of(block * rows, rows), rows)
+        query = qbuf[pl.ds(block * per, per)].reshape(rows, HD)
+        scores = lax.dot_general(query, key_block, (((1,), (1,)), ((), ())),
+                                 preferred_element_type=jnp.float32)
+        old = top_s[span, :]
+        new = jnp.maximum(old, jnp.max(scores, axis=1, keepdims=True))
+        top_s[span, :] = new
+        fade = jnp.exp2((old - new) * factor)
+        weights = [
+            jnp.exp2((scores[:, part * HD:(part + 1) * HD] - new) * factor)
+            for part in range(keys_each // HD)
+        ]
+        sum_s[span, :] = sum_s[span, :] * fade + functools.reduce(jnp.add, weights)
+        expo = jnp.concatenate([part.astype(jnp.bfloat16) for part in weights], axis=1)
+        acc_s[span, :] = acc_s[span, :] * fade + jnp.dot(
+            expo, value_block, preferred_element_type=jnp.float32)
+
+    def absorb(key_ref, value_ref):
         for block in range(HEADS // per):
-            span = pl.ds(block * rows, rows)
-            query = qbuf[pl.ds(block * per, per)].reshape(rows, HD)
-            scores = lax.dot_general(query, key_block, (((1,), (1,)), ((), ())),
-                                     preferred_element_type=jnp.float32)
-            old = top_s[span, :]
-            new = jnp.maximum(old, jnp.max(scores, axis=1, keepdims=True))
-            top_s[span, :] = new
-            fade = jnp.exp2((old - new) * factor)
-            weights = [
-                jnp.exp2((scores[:, part * HD:(part + 1) * HD] - new) * factor)
-                for part in range(keys_each // HD)
-            ]
-            sum_s[span, :] = sum_s[span, :] * fade + functools.reduce(jnp.add, weights)
-            expo = jnp.concatenate([part.astype(jnp.bfloat16) for part in weights], axis=1)
-            acc_s[span, :] = acc_s[span, :] * fade + jnp.dot(
-                expo, value_block, preferred_element_type=jnp.float32)
+            absorb_block(block, key_ref, value_ref)
 
     def forward(first, slot, dist, which):
         src, dst, recv = ((kbuf, kprior, kp_recv), (vbuf, vprior, vp_recv))[which]
@@ -134,16 +157,16 @@
             send_sem=fwd_send.at[which, dist - 1, slot], recv_sem=recv.at[dist - 1, slot],
             device_id=(stretch + dist, me), device_id_type=MESH)
 
-    my_chunk = me // chunk
-    low = my_chunk < chunks // 2
+    my_chunk = lax.div(me, chunk)
 
     def chunk_at(index):
-        rising = lax.rem(my_chunk + index, chunks)
-        falling = lax.rem(my_chunk + chunks - index, chunks)
-        return jnp.where(low, rising, falling)
-
-    @pl.loop(0, chunks)
-    def _(index):
+        slot = 0
+        for bit in range(chunks.bit_length() - 1):
+            step = 1 << bit
+            slot = slot + step * lax.rem(lax.div(my_chunk, step) + index // step, 2)
+        return slot
+
+    def take(index):
         slot = chunk_at(index)
         first = slot * chunk
         for step in range(chunk):
@@ -159,38 +182,59 @@
             def _():
                 forward(first, slot, dist, 0).start()
                 forward(first, slot, dist, 1).start()
-
-        absorb(kbuf.at[pl.ds(first, chunk)], vbuf.at[pl.ds(first, chunk)])
+        return slot, pl.ds(first, chunk)
+
+    def take_prior(dist, slot, part):
+        for src, recv in ((kprior, kp_recv), (vprior, vp_recv)):
+            pltpu.make_async_remote_copy(
+                src_ref=src.at[dist - 1, part], dst_ref=src.at[dist - 1, part],
+                send_sem=fwd_send.at[0, dist - 1, slot], recv_sem=recv.at[dist - 1, slot],
+                device_id=(stretch - dist, me), device_id_type=MESH).wait_recv()
+
+    @pl.loop(0, chunks - 1)
+    def _(index):
+        slot, part = take(index)
+        absorb(kbuf.at[part], vbuf.at[part])
         for dist in range(1, prior + 1):
             @pl.when(stretch >= dist)
             def _():
-                for which in range(2):
-                    src, recv = ((kprior, kp_recv), (vprior, vp_recv))[which]
-                    pltpu.make_async_remote_copy(
-                        src_ref=src.at[dist - 1, pl.ds(first, chunk)],
-                        dst_ref=src.at[dist - 1, pl.ds(first, chunk)],
-                        send_sem=fwd_send.at[which, dist - 1, slot], recv_sem=recv.at[dist - 1, slot],
-                        device_id=(stretch - dist, me), device_id_type=MESH).wait_recv()
-                absorb(kprior.at[dist - 1, pl.ds(first, chunk)], vprior.at[dist - 1, pl.ds(first, chunk)])
-
-    for source in range(HEADS):
-        span = pl.ds(source * count, count)
-        total = jnp.sum(sum_s[span, :], axis=1, keepdims=True)
-        obuf[source] = (acc_s[span, :] / total).astype(jnp.bfloat16)
-
-    def o_copy(off):
-        other = lax.rem(head + off, HEADS)
+                take_prior(dist, slot, part)
+                absorb(kprior.at[dist - 1, part], vprior.at[dist - 1, part])
+
+    def o_copy(other, slot):
         return pltpu.make_async_remote_copy(
             src_ref=obuf.at[other], dst_ref=att.at[:, cols(head)],
-            send_sem=o_send.at[other], recv_sem=o_recv.at[head],
+            send_sem=o_send.at[slot], recv_sem=o_recv.at[head],
             device_id=(stretch, share * HEADS + other), device_id_type=MESH)
 
-    @pl.loop(1, HEADS)
-    def _(off):
-        o_copy(off).start()
-
     own_out = pltpu.make_async_copy(obuf.at[head], att.at[:, cols(head)], local_sem.at[0])
-    own_out.start()
+    slot, part = take(chunks - 1)
+    absorb(kbuf.at[part], vbuf.at[part])
+    blocks = HEADS // per
+    home = lax.div(head, per)
+    sent = []
+    for turn in range(blocks):
+        block = lax.rem(home + 1 + turn, blocks)
+        for dist in range(1, prior + 1):
+            @pl.when(stretch >= dist)
+            def _():
+                if turn == 0:
+                    take_prior(dist, slot, part)
+                absorb_block(block, kprior.at[dist - 1, part], vprior.at[dist - 1, part])
+        for step in range(per):
+            source = block * per + step
+            span = pl.ds(pl.multiple_of(source * count, count), count)
+            total = jnp.sum(sum_s[span, :], axis=1, keepdims=True)
+            obuf[source] = (acc_s[span, :] / total).astype(jnp.bfloat16)
+        for step in range(per):
+            other = block * per + flip(lax.rem(head, per), step)
+            if turn == blocks - 1 and step == 0:
+                own_out.start()
+            else:
+                copy = o_copy(other, turn * per + step)
+                copy.start()
+                sent.append(copy)
+
     w_copy.wait()
     tok_copy.wait()
 
@@ -213,16 +257,13 @@
     normed = proj * lax.rsqrt(mean_sq + 1e-06)
     out_ref[...] = (tok_s[...].astype(jnp.float32) + gate * normed).astype(jnp.bfloat16)
 
-    @pl.loop(1, HEADS)
-    def _(off):
-        q_copy(off).wait_send()
-        o_copy(off).wait_send()
-
-    @pl.loop(0, groups - 1)
-    def _(index):
-        kv_copy(index, 0).wait_send()
-        kv_copy(index, 1).wait_send()
-
+    for copy in sent:
+        copy.wait_send()
+    for mask in range(1, groups):
+        if mask < HEADS:
+            q_copy(mask).wait_send()
+        kv_copy(mask, 0).wait_send()
+        kv_copy(mask, 1).wait_send()
     for dist in range(1, prior + 1):
         @pl.when(stretch + dist < stretches)
         def _():
@@ -274,6 +315,7 @@
                 dma((prior, groups // chunk)),
                 dma((HEADS,)),
                 dma((HEADS,)),
+                pltpu.SemaphoreType.REGULAR((max(1, groups.bit_length() - 1),)),
             ],
             compiler_params=pltpu.CompilerParams(collective_id=0, has_side_effects=True),
         )(queries, keys, values, tokens, out_weight, gate_table, timesteps)

time: 49 us -> 42.9 us (0.88)
  the two profiles are of different devices: /device:TPU:1 before, /device:TPU:0 now
where the time goes in v2:
time: 42.9 us; the launch traced here: 42.7 us
  Pallas kernels  40.3 us (94%)
  local copies, waits for them, and re-layouts  1.77 us (4%)
  between operations  0.66 us (2%)
    pallas_call x1, Pallas kernels, on_device(): pl.pallas_call(functools.partial(kernel, groups, stretches, chunk), out_s...  40.3 us
    unnamed x1, local copies, waits for them, and re-layouts  1.77 us

profile of v2, /device:TPU:0, one launch (start us, length us, event | category | flops | bytes accessed | tf_op | source)
XLA Modules:
  0.0 42.7 jit_solution(3006685977600280834)
XLA Ops:
  0.7 40.3 %shard_map.73 = bf16[128,1536]{1,0:T(8,128)(2,1)} custom-call(bf16[128,1024]{1,0:T(8,128)(2,1)} %q_ref.1, bf16[128,1024]{1,0:T(8,128)(2,1)} %k_ref.1, bf16[128,1024]{1,0:T(8,128)(2,1)} %v_ref.1, bf16[128,1536]{1,0:T(8,128)(2,1)} %tok_ref.1, bf16[1024,1536]{1,0:T(8,128)(2,1)} %w_ref.1, f32[4,1536]{1,0:T(4,128)} %gate_ref.1, s32[1]{0:T(128)S(6)} %copy.9.step_ref), custom_call_target="tpu_custom_call" | custom-call | tf_op jit(solution)/shard_map/pallas_call | solution.py:288
  40.9 1.8 %copy.10 = bf16[128,1536]{1,0:T(8,128)(2,1)} copy(bf16[128,1536]{1,0:T(8,128)(2,1)} %shard_map.73) | data formatting | bytes 786432

commit v3 on v2

--- a/solution.py
+++ b/solution.py
@@ -25,12 +25,12 @@
 
 def rounds_of(bits):
     known = {0} | {1 << bit for bit in range(bits)}
-    rounds = [sorted(known - {0}, reverse=True)]
+    rounds = [sorted(known - {0})]
     for bit in range(bits):
         fresh = {mask ^ (1 << bit) for mask in known} - known
         if not fresh:
             break
-        rounds.append(sorted(fresh, reverse=True))
+        rounds.append(sorted(fresh))
         known |= fresh
     return rounds
 
@@ -243,16 +243,20 @@
     gate = jnp.sum(jnp.where(picked, table, 0.0), axis=0, keepdims=True)
 
     own_out.wait()
-
-    @pl.loop(1, HEADS)
-    def _(off):
-        other = lax.rem(head + off, HEADS)
-        pltpu.make_async_remote_copy(
-            src_ref=obuf.at[other], dst_ref=att.at[:, cols(other)],
-            send_sem=o_send.at[other], recv_sem=o_recv.at[other],
-            device_id=(stretch, share * HEADS + other), device_id_type=MESH).wait_recv()
-
-    proj = jnp.dot(att[...], w_s[...], preferred_element_type=jnp.float32)
+    for step in range(HEADS):
+        mask = step
+        if mask:
+            other = flip(head, mask)
+            pltpu.make_async_remote_copy(
+                src_ref=obuf.at[other], dst_ref=att.at[:, cols(other)],
+                send_sem=o_send.at[0], recv_sem=o_recv.at[other],
+                device_id=(stretch, share * HEADS + other), device_id_type=MESH).wait_recv()
+        if step % per == per - 1:
+            wide = per * HD
+            base = pl.multiple_of(lax.div(flip(head, step), per) * wide, wide)
+            term = jnp.dot(att[:, pl.ds(base, wide)], w_s[pl.ds(base, wide), :],
+                           preferred_element_type=jnp.float32)
+            proj = term if step < per else proj + term
     mean_sq = jnp.mean(proj * proj, axis=1, keepdims=True)
     normed = proj * lax.rsqrt(mean_sq + 1e-06)
     out_ref[...] = (tok_s[...].astype(jnp.float32) + gate * normed).astype(jnp.bfloat16)

time: 42.9 us -> 42.8 us (level)
  no operation moved by 1% of the time
where the time goes in v3:
time: 42.8 us; the launch traced here: 42.5 us
  Pallas kernels  40.1 us (94%)
  local copies, waits for them, and re-layouts  1.77 us (4%)
  between operations  0.66 us (2%)
    pallas_call x1, Pallas kernels, on_device(): pl.pallas_call(functools.partial(kernel, groups, stretches, chunk), out_s...  40.1 us
    unnamed x1, local copies, waits for them, and re-layouts  1.77 us

profile of v3, /device:TPU:0, one launch (start us, length us, event | category | flops | bytes accessed | tf_op | source)
XLA Modules:
  0.0 42.5 jit_solution(16816780454783338705)
XLA Ops:
  0.7 40.1 %shard_map.73 = bf16[128,1536]{1,0:T(8,128)(2,1)} custom-call(bf16[128,1024]{1,0:T(8,128)(2,1)} %q_ref.1, bf16[128,1024]{1,0:T(8,128)(2,1)} %k_ref.1, bf16[128,1024]{1,0:T(8,128)(2,1)} %v_ref.1, bf16[128,1536]{1,0:T(8,128)(2,1)} %tok_ref.1, bf16[1024,1536]{1,0:T(8,128)(2,1)} %w_ref.1, f32[4,1536]{1,0:T(4,128)} %gate_ref.1, s32[1]{0:T(128)S(6)} %copy.9.step_ref), custom_call_target="tpu_custom_call" | custom-call | tf_op jit(solution)/shard_map/pallas_call | solution.py:292
  40.8 1.8 %copy.10 = bf16[128,1536]{1,0:T(8,128)(2,1)} copy(bf16[128,1536]{1,0:T(8,128)(2,1)} %shard_map.73) | data formatting | bytes 786432
